TPU v7x, 32 devices: a whole 2x2x4 slice. The times are simulated.
32 devices in a mesh: dp: 8 (over y, x, core), expert: 4 (over z).
Axes of the slice: x: 2, y: 2, z: 4, core: 2. Of those that a mesh axis runs over, the one named last changes fastest.
Arguments:
- tokens: bfloat16 [4096, 2048], P(('dp', 'expert')), may hold values from -6 to 6
- routes: int32 [4096, 2], P(('dp', 'expert')), may hold values from 0 to 3, all different within a row; in each aligned block of 128 rows (0 to 127, 128 to 255, ...) at most 80 rows name the same one
- gates: float32 [4096, 2], P(('dp', 'expert')), may hold values from 0.2 to 1
- cotangent: bfloat16 [4096, 2048], P(('dp', 'expert')), may hold values from -6 to 6
- w_gate: bfloat16 [4, 2048, 384], P('expert', 'dp'), may hold values from -0.125 to 0.125
- w_up: bfloat16 [4, 2048, 384], P('expert', 'dp'), may hold values from -0.125 to 0.125
- w_down: bfloat16 [4, 384, 2048], P('expert', None, 'dp'), may hold values from -0.3125 to 0.3125
Outputs:
- mixed: bfloat16 [4096, 2048], P(('dp', 'expert'))
- token_grads: bfloat16 [4096, 2048], P(('dp', 'expert'))
- gate_grads: float32 [4096, 2], P(('dp', 'expert'))
- grad_gate: float32 [4, 2048, 384], P('expert', 'dp')
- grad_up: float32 [4, 2048, 384], P('expert', 'dp')
- grad_down: float32 [4, 384, 2048], P('expert', None, 'dp')
Inputs may be any that keep to these rules, and one draw needn't show every extreme that they name: `routes`: each row names 2 different experts. Within the 128 rows of one device no expert is named by more than 80 rows, a bound that some expert reaches in some device's rows.
All inputs are finite; a program needn't handle non-finite values.
Results may differ from a plain program's by a relative error of at most 0.015.
Values may be sent and summed in bfloat16 or wider, within the bound.
A program may use at most 64 MiB of HBM per device.

v0:
```python
import jax
import jax.numpy as jnp
from jax import lax
from jax.sharding import PartitionSpec as P


def contract_last(left, right):
    return lax.dot_general(
        left, right, (((1,), (1,)), ((), ())), preferred_element_type=jnp.float32
    )


def contract_first(left, right):
    return lax.dot_general(
        left, right, (((0,), (0,)), ((), ())), preferred_element_type=jnp.float32
    )


def body(tokens, routes, gates, cotangent, w_gate, w_up, w_down):
    experts = lax.axis_size("expert")
    token_rows = tokens.shape[0]
    picks = routes.shape[1]
    width = tokens.shape[1]
    capacity = max(2, 5 * token_rows * picks // (4 * experts))
    entries = token_rows * picks
    slot_count = experts * capacity
    flat_routes = routes.reshape(entries)
    member = (flat_routes[:, None] == jnp.arange(experts, dtype=jnp.int32)[None, :]).astype(
        jnp.int32
    )
    earlier = jnp.cumsum(member, axis=0) - member
    target = flat_routes * capacity + jnp.sum(earlier * member, axis=1)
    placing = (jnp.arange(slot_count, dtype=jnp.int32)[:, None] == target[None, :]).astype(
        jnp.bfloat16
    )
    placing_tokens = jnp.sum(placing.reshape(slot_count, token_rows, picks), axis=2)
    outbound = jnp.dot(placing_tokens, tokens, preferred_element_type=jnp.float32).astype(
        jnp.bfloat16
    )
    outbound = outbound.reshape(experts, capacity, width)
    scaled = (gates[:, :, None] * cotangent.astype(jnp.float32)[:, None, :]).astype(jnp.bfloat16)
    grad_outbound = jnp.dot(
        placing, scaled.reshape(entries, width), preferred_element_type=jnp.float32
    )
    grad_outbound = grad_outbound.astype(jnp.bfloat16).reshape(experts, capacity, width)
    inbound = lax.all_to_all(outbound, "expert", split_axis=0, concat_axis=0, tiled=True)
    slot_rows = inbound.reshape(slot_count, width)
    full_gate, full_up, full_down = (
        lax.all_gather(w_gate, "dp", axis=1, tiled=True),
        lax.all_gather(w_up, "dp", axis=1, tiled=True),
        lax.all_gather(w_down, "dp", axis=2, tiled=True),
    )
    full_gate = full_gate[0]
    full_up = full_up[0]
    full_down = full_down[0]
    gate_pre = jnp.dot(slot_rows, full_gate, preferred_element_type=jnp.float32)
    up_pre = jnp.dot(slot_rows, full_up, preferred_element_type=jnp.float32)
    sigma = jax.nn.sigmoid(gate_pre)
    swish = gate_pre * sigma
    hidden = (swish * up_pre).astype(jnp.bfloat16)
    expert_out = jnp.dot(hidden, full_down, preferred_element_type=jnp.float32).astype(jnp.bfloat16)
    returned = lax.all_to_all(
        expert_out.reshape(experts, capacity, width),
        "expert",
        split_axis=0,
        concat_axis=0,
        tiled=True,
    )
    per_entry = contract_first(placing, returned.reshape(slot_count, width)).reshape(
        token_rows, picks, width
    )
    mixed = jnp.sum(gates[:, :, None] * per_entry, axis=1).astype(jnp.bfloat16)
    gate_grads = jnp.sum(cotangent.astype(jnp.float32)[:, None, :] * per_entry, axis=2)
    grad_inbound = lax.all_to_all(grad_outbound, "expert", split_axis=0, concat_axis=0, tiled=True)
    grad_rows = grad_inbound.reshape(slot_count, width)
    d_hidden = contract_last(grad_rows, full_down)
    d_gate = (d_hidden * up_pre * sigma * (1.0 + gate_pre * (1.0 - sigma))).astype(jnp.bfloat16)
    d_up = (d_hidden * swish).astype(jnp.bfloat16)
    part_gate = contract_first(slot_rows, d_gate)
    part_up = contract_first(slot_rows, d_up)
    part_down = contract_first(hidden, grad_rows)
    shares = (
        lax.psum_scatter(
            part_gate.astype(jnp.bfloat16), "dp", scatter_dimension=0, tiled=True
        ).astype(jnp.float32),
        lax.psum_scatter(
            part_up.astype(jnp.bfloat16), "dp", scatter_dimension=0, tiled=True
        ).astype(jnp.float32),
        lax.psum_scatter(
            part_down.astype(jnp.bfloat16), "dp", scatter_dimension=1, tiled=True
        ).astype(jnp.float32),
    )
    entry_grad = (contract_last(d_gate, full_gate) + contract_last(d_up, full_up)).astype(
        jnp.bfloat16
    )
    arrived = lax.all_to_all(
        entry_grad.reshape(experts, capacity, width),
        "expert",
        split_axis=0,
        concat_axis=0,
        tiled=True,
    )
    token_grads = contract_first(placing_tokens, arrived.reshape(slot_count, width)).astype(
        jnp.bfloat16
    )
    return (mixed, token_grads, gate_grads, shares[0][None], shares[1][None], shares[2][None])


def solution(mesh):
    return jax.shard_map(
        body,
        mesh=mesh,
        in_specs=(
            P(("dp", "expert"), None),
            P(("dp", "expert"), None),
            P(("dp", "expert"), None),
            P(("dp", "expert"), None),
            P("expert", "dp", None),
            P("expert", "dp", None),
            P("expert", None, "dp"),
        ),
        out_specs=(
            P(("dp", "expert"), None),
            P(("dp", "expert"), None),
            P(("dp", "expert"), None),
            P("expert", "dp", None),
            P("expert", "dp", None),
            P("expert", None, "dp"),
        ),
        check_vma=False,
    )
```

profile of v0, /device:TPU:0, one launch (start us, length us, event | category | flops | bytes accessed | tf_op | source)
XLA Modules:
  0.0 229.6 jit_solution(18241620535647696961)
XLA Ops:
  13.9 6.5 %all-to-all-start = ((bf16[4,80,2048]{2,1,0:T(8,128)(2,1)}), bf16[4,80,2048]{2,1,0:T(8,128)(2,1)}, u32[]{:S(2)}, u32[]{:S(2)}) async-start(bf16[4,80,2048]{2,1,0:T(8,128)(2,1)} %bitcast.2), calls=%async_computation | async-start | bytes 2621440 | tf_op jit(solution)/shard_map/all_to_all | solution.py:46
  22.2 2.5 %mul.83 = f32[256,2048]{1,0:T(8,128)} reshape(f32[128,2,2048]{2,1,0:T(2,128)S(1)} %mul.82.clone) | data formatting | bytes 4194304 | tf_op jit(solution)/shard_map/mul | solution.py:41
  24.9 3.2 %convolution_convert_fusion.4 = bf16[320,2048]{1,0:T(8,128)(2,1)} fusion(f32[256,2048]{1,0:T(8,128)} %mul.83, f32[256]{0:T(256)S(1)} %mul.80, s32[256]{0:T(256)S(1)} %multiply_add_fusion.1), kind=kOutput, calls=%fused_computation.6 | convolution fusion | flops 337330176 | bytes 3409920 | tf_op jit(solution)/shard_map/dot_general | solution.py:42
  28.2 23.7 %all-to-all-done = bf16[4,80,2048]{2,1,0:T(8,128)(2,1)} async-done(((bf16[4,80,2048]{2,1,0:T(8,128)(2,1)}), bf16[4,80,2048]{2,1,0:T(8,128)(2,1)}, u32[]{:S(2)}, u32[]{:S(2)}) %all-to-all-start) | async-done | bytes 1310752 | tf_op jit(solution)/shard_map/all_to_all | solution.py:46
  51.9 3.5 %all-to-all-start.2 = ((bf16[4,80,2048]{2,1,0:T(8,128)(2,1)}), bf16[4,80,2048]{2,1,0:T(8,128)(2,1)S(1)}, u32[]{:S(2)}, u32[]{:S(2)}) async-start(bf16[4,80,2048]{2,1,0:T(8,128)(2,1)} %bitcast.10), calls=%async_computation.2 | async-start | bytes 2621440 | tf_op jit(solution)/shard_map/all_to_all | solution.py:74
  55.5 2.7 %fusion.9 = f32[320,384]{1,0:T(8,128)S(1)} fusion(bf16[320,2048]{1,0:T(8,128)(2,1)} %bitcast.3, bf16[1,2048,384]{2,1,0:T(8,128)(2,1)} %all-gather.4.cloned.1.call-done), kind=kOutput, calls=%fused_computation.20 | convolution fusion | flops 503316480 | bytes 3375104 | tf_op jit(solution)/shard_map/dot_general | solution.py:56
  58.1 7.6 %all-gather.6.cloned.1.call-done = bf16[1,2048,384]{2,1,0:T(8,128)(2,1)} async-done(((bf16[1,256,384]{2,1,0:T(8,128)(2,1)}), bf16[1,2048,384]{2,1,0:T(8,128)(2,1)}) %all-gather.6.cloned.1.call-update) | async-done | bytes 1572880 | tf_op jit(solution)/shard_map/all_gather | solution.py:50
  65.7 3.4 %fusion.5 = f32[320,384]{1,0:T(8,128)} fusion(bf16[320,2048]{1,0:T(8,128)(2,1)} %bitcast.3, bf16[1,2048,384]{2,1,0:T(8,128)(2,1)} %all-gather.6.cloned.1.call-done), kind=kOutput, calls=%fused_computation.16 | convolution fusion | flops 503316480 | bytes 3375104 | tf_op jit(solution)/shard_map/dot_general | solution.py:57
  69.2 17.1 %all-to-all-done.2 = bf16[4,80,2048]{2,1,0:T(8,128)(2,1)S(1)} async-done(((bf16[4,80,2048]{2,1,0:T(8,128)(2,1)}), bf16[4,80,2048]{2,1,0:T(8,128)(2,1)S(1)}, u32[]{:S(2)}, u32[]{:S(2)}) %all-to-all-start.2) | async-done | bytes 1310752 | tf_op jit(solution)/shard_map/all_to_all | solution.py:74
  86.3 7.2 %all-gather.8.cloned.1.call-done = bf16[1,384,2048]{2,1,0:T(8,128)(2,1)} async-done(((bf16[1,384,256]{2,1,0:T(8,128)(2,1)}), bf16[1,384,2048]{2,1,0:T(8,128)(2,1)}) %all-gather.8.cloned.1.call-update) | async-done | bytes 1572880 | tf_op jit(solution)/shard_map/all_gather | solution.py:51
  93.4 2.5 %multiply_convert_fusion.2 = (bf16[320,384]{1,0:T(8,128)(2,1)S(1)}, bf16[320,384]{1,0:T(8,128)(2,1)S(1)}, bf16[320,384]{1,0:T(8,128)(2,1)S(1)}) fusion(f32[320,384]{1,0:T(8,128)S(1)} %fusion.9, f32[320,384]{1,0:T(8,128)} %fusion.5, bf16[320,2048]{1,0:T(8,128)(2,1)S(1)} %bitcast.72, bf16[1,384,2048]{2,1,0:T(8,128)(2,1)} %all-gather.8.cloned.1.call-done), kind=kOutput, calls=%fused_computation.23 | convolution fusion | flops 505159680 | bytes 4603904 | tf_op jit(solution)/shard_map/dot_general | solution.py:8
  95.9 3.6 %convolution_convert_fusion.2 = bf16[2048,384]{1,0:T(8,128)(2,1)} fusion(bf16[320,2048]{1,0:T(8,128)(2,1)} %bitcast.3, bf16[320,384]{1,0:T(8,128)(2,1)S(1)} %get-tuple-element.9), kind=kOutput, calls=%fused_computation.3 | convolution fusion | flops 504102912 | bytes 3129344 | tf_op jit(solution)/shard_map/dot_general | solution.py:14
  99.6 3.6 %convolution_convert_fusion.1 = bf16[2048,384]{1,0:T(8,128)(2,1)} fusion(bf16[320,2048]{1,0:T(8,128)(2,1)} %bitcast.3, bf16[320,384]{1,0:T(8,128)(2,1)S(1)} %get-tuple-element.8), kind=kOutput, calls=%fused_computation.2 | convolution fusion | flops 504102912 | bytes 3129344 | tf_op jit(solution)/shard_map/dot_general | solution.py:14
  103.3 2.4 %fusion.7 = f32[320,2048]{1,0:T(8,128)S(1)} fusion(bf16[320,384]{1,0:T(8,128)(2,1)S(1)} %get-tuple-element.9, bf16[1,2048,384]{2,1,0:T(8,128)(2,1)} %all-gather.4.cloned.1.call-done), kind=kOutput, calls=%fused_computation.18 | convolution fusion | flops 503316480 | bytes 4440064 | tf_op jit(solution)/shard_map/dot_general | solution.py:8
  105.7 2.0 fusion
  107.7 4.6 %all-to-all-start.3 = ((bf16[4,80,2048]{2,1,0:T(8,128)(2,1)}), bf16[4,80,2048]{2,1,0:T(8,128)(2,1)S(1)}, u32[]{:S(2)}, u32[]{:S(2)}) async-start(bf16[4,80,2048]{2,1,0:T(8,128)(2,1)} %bitcast.75), calls=%async_computation.3 | async-start | bytes 2621440 | tf_op jit(solution)/shard_map/all_to_all | solution.py:96
  112.3 3.4 %convolution_convert_fusion.5 = bf16[320,2048]{1,0:T(8,128)(2,1)} fusion(bf16[320,384]{1,0:T(8,128)(2,1)S(1)} %get-tuple-element.10, bf16[1,384,2048]{2,1,0:T(8,128)(2,1)} %all-gather.8.cloned.1.call-done), kind=kOutput, calls=%fused_computation.7 | convolution fusion | flops 503971840 | bytes 3129344 | tf_op jit(solution)/shard_map/dot_general | solution.py:61
  115.6 28.4 %all-to-all-done.3 = bf16[4,80,2048]{2,1,0:T(8,128)(2,1)S(1)} async-done(((bf16[4,80,2048]{2,1,0:T(8,128)(2,1)}), bf16[4,80,2048]{2,1,0:T(8,128)(2,1)S(1)}, u32[]{:S(2)}, u32[]{:S(2)}) %all-to-all-start.3) | async-done | bytes 1310752 | tf_op jit(solution)/shard_map/all_to_all | solution.py:96
  144.0 4.3 %all-to-all-start.1 = ((bf16[4,80,2048]{2,1,0:T(8,128)(2,1)}), bf16[4,80,2048]{2,1,0:T(8,128)(2,1)}, u32[]{:S(2)}, u32[]{:S(2)}) async-start(bf16[4,80,2048]{2,1,0:T(8,128)(2,1)} %bitcast.7), calls=%async_computation.1 | async-start | bytes 2621440 | tf_op jit(solution)/shard_map/all_to_all | solution.py:62
  148.6 2.2 convolution_convert_fusion
  154.6 24.8 %all-to-all-done.1 = bf16[4,80,2048]{2,1,0:T(8,128)(2,1)} async-done(((bf16[4,80,2048]{2,1,0:T(8,128)(2,1)}), bf16[4,80,2048]{2,1,0:T(8,128)(2,1)}, u32[]{:S(2)}, u32[]{:S(2)}) %all-to-all-start.1) | async-done | bytes 1310752 | tf_op jit(solution)/shard_map/all_to_all | solution.py:62
  179.3 3.1 %multiply_reduce_fusion = (f32[128,2]{0,1:T(2,128)}, bf16[128,2048]{1,0:T(8,128)(2,1)}) fusion(f32[128,2048]{1,0:T(8,128)S(1)} %copy-done.4, f32[128,2]{0,1:T(2,128)S(1)} %copy-done.5, bf16[320,2048,1]{1,0,2:T(8,128)(2,1)} %bitcast.9, pred[128,2,320]{2,1,0:T(4,128)(4,1)S(1)} %eq.68), kind=kOutput, calls=%fused_computation.9 | convolution fusion | flops 337379072 | bytes 2967552 | tf_op jit(solution)/shard_map/dot_general | solution.py:14
  182.4 1.7 bitcast_convert_fusion.2
  185.8 35.2 %reduce-scatter.8.cloned.1.call-done = bf16[384,256]{1,0:T(8,128)(2,1)} async-done(((bf16[384,2048]{1,0:T(8,128)(2,1)}), bf16[384,256]{1,0:T(8,128)(2,1)}) %reduce-scatter.8.cloned.1.call-update) | async-done | bytes 196624 | tf_op jit(solution)/shard_map/reduce_scatter | solution.py:89
  (54 shorter events, 16.2 us)
Async XLA Ops:
  7.2 5.2 %copy-start = (bf16[128,2048]{1,0:T(8,128)(2,1)S(1)}, bf16[128,2048]{1,0:T(8,128)(2,1)}, u32[]{:S(2)}) copy-start(bf16[128,2048]{1,0:T(8,128)(2,1)} %param.7) | copy-start | bytes 1572868
  7.2 48.3 %all-gather.4.cloned.1.call-start = ((), (), s32[]{:S(2)}) async-start(), calls=%async_computation.7 | async-start | bytes 1769472 | tf_op jit(solution)/shard_map/all_gather | solution.py:49
  7.9 57.8 %all-gather.6.cloned.1.call-start = ((), (), s32[]{:S(2)}) async-start(), calls=%async_computation.8 | async-start | bytes 1769472 | tf_op jit(solution)/shard_map/all_gather | solution.py:50
  13.9 7.2 %copy-start.1 = (bf16[128,2048]{1,0:T(8,128)(2,1)S(1)}, bf16[128,2048]{1,0:T(8,128)(2,1)}, u32[]{:S(2)}) copy-start(bf16[128,2048]{1,0:T(8,128)(2,1)} %param.10) | copy-start | bytes 1572868
  13.9 37.9 %all-to-all-start = ((bf16[4,80,2048]{2,1,0:T(8,128)(2,1)}), bf16[4,80,2048]{2,1,0:T(8,128)(2,1)}, u32[]{:S(2)}, u32[]{:S(2)}) async-start(bf16[4,80,2048]{2,1,0:T(8,128)(2,1)} %bitcast.2), calls=%async_computation | async-start | bytes 2621440 | tf_op jit(solution)/shard_map/all_to_all | solution.py:46
  20.4 73.0 %all-gather.8.cloned.1.call-start = ((), (), s32[]{:S(2)}) async-start(), calls=%async_computation.9 | async-start | bytes 1769472 | tf_op jit(solution)/shard_map/all_gather | solution.py:51
  22.2 2.5 %copy-start.5 = (f32[128,2]{0,1:T(2,128)S(1)}, f32[128,2]{0,1:T(2,128)}, u32[]{:S(2)}) copy-start(f32[128,2]{0,1:T(2,128)} %param.9) | copy-start | bytes 3076
  51.9 34.4 %all-to-all-start.2 = ((bf16[4,80,2048]{2,1,0:T(8,128)(2,1)}), bf16[4,80,2048]{2,1,0:T(8,128)(2,1)S(1)}, u32[]{:S(2)}, u32[]{:S(2)}) async-start(bf16[4,80,2048]{2,1,0:T(8,128)(2,1)} %bitcast.10), calls=%async_computation.2 | async-start | bytes 2621440 | tf_op jit(solution)/shard_map/all_to_all | solution.py:74
  55.4 127.0 %reduce-scatter.4.cloned.1.call-start = ((), (), s32[]{:S(2)}) async-start(), calls=%async_computation.10 | async-start | bytes 1769472 | tf_op jit(solution)/shard_map/reduce_scatter | solution.py:83
  99.5 84.6 %reduce-scatter.6.cloned.1.call-start = ((), (), s32[]{:S(2)}) async-start(), calls=%async_computation.11 | async-start | bytes 1769472 | tf_op jit(solution)/shard_map/reduce_scatter | solution.py:86
  103.3 2.4 %copy-start.3 = (bf16[1,2048,384]{2,1,0:T(8,128)(2,1)S(1)}, bf16[1,2048,384]{2,1,0:T(8,128)(2,1)}, u32[]{:S(2)}) copy-start(bf16[1,2048,384]{2,1,0:T(8,128)(2,1)} %all-gather.6.cloned.1.call-done) | copy-start | bytes 4718596
  107.7 36.4 %all-to-all-start.3 = ((bf16[4,80,2048]{2,1,0:T(8,128)(2,1)}), bf16[4,80,2048]{2,1,0:T(8,128)(2,1)S(1)}, u32[]{:S(2)}, u32[]{:S(2)}) async-start(bf16[4,80,2048]{2,1,0:T(8,128)(2,1)} %bitcast.75), calls=%async_computation.3 | async-start | bytes 2621440 | tf_op jit(solution)/shard_map/all_to_all | solution.py:96
  144.0 35.3 %all-to-all-start.1 = ((bf16[4,80,2048]{2,1,0:T(8,128)(2,1)}), bf16[4,80,2048]{2,1,0:T(8,128)(2,1)}, u32[]{:S(2)}, u32[]{:S(2)}) async-start(bf16[4,80,2048]{2,1,0:T(8,128)(2,1)} %bitcast.7), calls=%async_computation.1 | async-start | bytes 2621440 | tf_op jit(solution)/shard_map/all_to_all | solution.py:62
  148.4 72.7 %reduce-scatter.8.cloned.1.call-start = ((), (), s32[]{:S(2)}) async-start(), calls=%async_computation.12 | async-start | bytes 1769472 | tf_op jit(solution)/shard_map/reduce_scatter | solution.py:89
  150.8 1.1 copy-start.2
  153.0 26.3 %copy-start.4 = (f32[128,2048]{1,0:T(8,128)S(1)}, f32[128,2048]{1,0:T(8,128)}, u32[]{:S(2)}) copy-start(f32[128,2048]{1,0:T(8,128)} %convert_element_type.67) | copy-start | bytes 3145732
Sparse Core Ops, SparseCore 0:
  9.9 28.3 all-gather.3
  40.1 25.5 all-gather.5
  67.6 25.7 all-gather.7
  99.7 38.3 reduce-scatter.3
  141.2 38.3 reduce-scatter.5
  182.7 38.3 reduce-scatter.7
where the time goes:
time: 230 us
  waiting for transfers between devices  146 us (63%)
  matrix products  34.9 us (15%)
  starting transfers between devices  19.3 us (8%)
  between operations  14.3 us (6%)
  other arithmetic  8.5 us (4%)
  local copies, waits for them, and re-layouts  6.49 us (3%)
    reduce_scatter x1, waiting for transfers between devices, body(): lax.psum_scatter(part_down.astype(jnp.bfloat16), 'dp', scatter_dimension=...  35.2 us
    all_to_all x1, waiting for transfers between devices, body(): lax.all_to_all(entry_grad.reshape(experts, capacity, width), 'expert', sp...  28.4 us
    all_to_all x1, waiting for transfers between devices, body(): lax.all_to_all(expert_out.reshape(experts, capacity, width), 'expert', sp...  24.8 us
    all_to_all x1, waiting for transfers between devices, body(): lax.all_to_all(outbound, 'expert', split_axis=0, concat_axis=0, tiled=True)  23.7 us
    all_to_all x1, waiting for transfers between devices, body(): lax.all_to_all(grad_outbound, 'expert', split_axis=0, concat_axis=0, tile...  17.1 us
    dot_general x5, matrix products, contract_first(): lax.dot_general(left, right, (((0,), (0,)), ((), ())), preferred_element_...  13.9 us
    all_gather x1, waiting for transfers between devices, body(): lax.all_gather(w_up, 'dp', axis=1, tiled=True)  7.58 us
    all_gather x1, waiting for transfers between devices, body(): lax.all_gather(w_down, 'dp', axis=2, tiled=True)  7.16 us
  transfers between devices with their start and end apart: 10, of which 7 were waited for; matrix products, arithmetic and copies ran while one was open for 18% of the time, Pallas kernels for 0%

commit v1 on v0

--- a/solution.py
+++ b/solution.py
@@ -2,6 +2,22 @@
 import jax.numpy as jnp
 from jax import lax
 from jax.sharding import PartitionSpec as P
+
+
+def pairwise_exchange(value, axis, split, join):
+    ways, here = (lax.axis_size(axis), lax.axis_index(axis))
+    width = value.shape[split] // ways
+    lengths = list(value.shape)
+    lengths[split] = width
+    height = lengths[join]
+    lengths[join] = height * ways
+    full = jnp.zeros(lengths, value.dtype)
+    for mask in range(ways):
+        part = lax.dynamic_slice_in_dim(value, (here ^ mask) * width, width, axis=split)
+        if mask:
+            part = lax.ppermute(part, axis, [(d, d ^ mask) for d in range(ways)])
+        full = lax.dynamic_update_slice_in_dim(full, part, (here ^ mask) * height, axis=join)
+    return full
 
 
 def contract_last(left, right):
@@ -71,7 +87,7 @@
     )
     mixed = jnp.sum(gates[:, :, None] * per_entry, axis=1).astype(jnp.bfloat16)
     gate_grads = jnp.sum(cotangent.astype(jnp.float32)[:, None, :] * per_entry, axis=2)
-    grad_inbound = lax.all_to_all(grad_outbound, "expert", split_axis=0, concat_axis=0, tiled=True)
+    grad_inbound = pairwise_exchange(grad_outbound, "expert", 0, 0)
     grad_rows = grad_inbound.reshape(slot_count, width)
     d_hidden = contract_last(grad_rows, full_down)
     d_gate = (d_hidden * up_pre * sigma * (1.0 + gate_pre * (1.0 - sigma))).astype(jnp.bfloat16)

time: 230 us -> 229 us (level)
    ppermute x0 -> x3, waiting for transfers between devices: none -> 42.6 us  [pairwise_exchange(): part = lax.ppermute(part, axis, [(d, d ^ mask) for d in range(ways)])]
    reduce_scatter x1, waiting for transfers between devices: 35.2 us -> 0.01 us  [body(): lax.psum_scatter(part_down.astype(jnp.bfloat16), 'dp', scatter_dimension=...]
    reduce_scatter x1, waiting for transfers between devices: 0.01 us -> 34.4 us  [body(): lax.psum_scatter(part_gate.astype(jnp.bfloat16), 'dp', scatter_dimension=...]
    all_to_all x1, waiting for transfers between devices: 23.7 us -> 0.01 us  [body(): lax.all_to_all(outbound, 'expert', split_axis=0, concat_axis=0, tiled=True)]
    all_to_all x1 -> x0, waiting for transfers between devices: 17.1 us -> none  [body(): lax.all_to_all(grad_outbound, 'expert', split_axis=0, concat_axis=0, tile...]
    all_gather x1, waiting for transfers between devices: 7.58 us -> 0.02 us  [body(): lax.all_gather(w_up, 'dp', axis=1, tiled=True)]
    all_gather x1, waiting for transfers between devices: 7.16 us -> 11.9 us  [body(): lax.all_gather(w_down, 'dp', axis=2, tiled=True)]
    ppermute x0 -> x3, starting transfers between devices: none -> 4.53 us  [pairwise_exchange(): part = lax.ppermute(part, axis, [(d, d ^ mask) for d in range(ways)])]
  transfers between devices with their start and end apart: 10 -> 12, of which waited for: 7 -> 6; matrix products, arithmetic and copies ran while one was open for 18% -> 18% of each run, Pallas kernels for 0% -> 0%
where the time goes in v1:
time: 229 us; the launch traced here: 228 us
  waiting for transfers between devices  144 us (63%)
  matrix products  33.7 us (15%)
  starting transfers between devices  20.4 us (9%)
  between operations  14.3 us (6%)
  other arithmetic  8.42 us (4%)
  local copies, waits for them, and re-layouts  7.75 us (3%)
    ppermute x3, waiting for transfers between devices, pairwise_exchange(): part = lax.ppermute(part, axis, [(d, d ^ mask) for d in range(ways)])  42.6 us
    reduce_scatter x1, waiting for transfers between devices, body(): lax.psum_scatter(part_gate.astype(jnp.bfloat16), 'dp', scatter_dimension=...  34.4 us
    all_to_all x1, waiting for transfers between devices, body(): lax.all_to_all(entry_grad.reshape(experts, capacity, width), 'expert', sp...  28.4 us
    all_to_all x1, waiting for transfers between devices, body(): lax.all_to_all(expert_out.reshape(experts, capacity, width), 'expert', sp...  24.3 us
    dot_general x5, matrix products, contract_first(): lax.dot_general(left, right, (((0,), (0,)), ((), ())), preferred_element_...  14.2 us
    all_gather x1, waiting for transfers between devices, body(): lax.all_gather(w_down, 'dp', axis=2, tiled=True)  11.9 us
    all_to_all x1, starting transfers between devices, body(): lax.all_to_all(outbound, 'expert', split_axis=0, concat_axis=0, tiled=True)  6.48 us
    dot_general x3, matrix products, contract_last(): lax.dot_general(left, right, (((1,), (1,)), ((), ())), preferred_element_...  5.53 us
  transfers between devices with their start and end apart: 12, of which 6 were waited for; matrix products, arithmetic and copies ran while one was open for 18% of the time, Pallas kernels for 0%

profile of v1, /device:TPU:0, one launch (start us, length us, event | category | flops | bytes accessed | tf_op | source)
XLA Modules:
  0.0 228.3 jit_solution(6371304609010237357)
XLA Ops:
  14.7 6.5 %all-to-all-start = ((bf16[4,80,2048]{2,1,0:T(8,128)(2,1)}), bf16[4,80,2048]{2,1,0:T(8,128)(2,1)}, u32[]{:S(2)}, u32[]{:S(2)}) async-start(bf16[4,80,2048]{2,1,0:T(8,128)(2,1)} %bitcast.2), calls=%async_computation | async-start | bytes 2621440 | tf_op jit(solution)/shard_map/all_to_all | solution.py:62
  22.2 2.5 %mul.83 = f32[256,2048]{1,0:T(8,128)} reshape(f32[128,2,2048]{2,1,0:T(2,128)S(1)} %mul.82.clone) | data formatting | bytes 4194304 | tf_op jit(solution)/shard_map/mul | solution.py:57
  24.9 2.2 convolution_convert_fusion.4
  27.4 2.1 collective-permute-start
  29.5 2.4 %collective-permute-start.1 = (bf16[1,80,2048]{2,1,0:T(8,128)(2,1)S(1)}, bf16[1,80,2048]{2,1,0:T(8,128)(2,1)S(1)}, u32[]{:S(2)}, u32[]{:S(2)}) collective-permute-start(bf16[1,80,2048]{2,1,0:T(8,128)(2,1)S(1)} %get-tuple-element.9), channel_id=1, source_target_pairs={{0,2},{1,3},{2,0},{3,1},{4,6},{5,7},{6,4},{7,5},{8,10},{9,11},{10,... | collective-permute-start | bytes 983048 | tf_op jit(solution)/shard_map/ppermute | solution.py:18
  31.9 18.6 %collective-permute-done = bf16[1,80,2048]{2,1,0:T(8,128)(2,1)S(1)} collective-permute-done((bf16[1,80,2048]{2,1,0:T(8,128)(2,1)S(1)}, bf16[1,80,2048]{2,1,0:T(8,128)(2,1)S(1)}, u32[]{:S(2)}, u32[]{:S(2)}) %collective-permute-start) | collective-permute-done | bytes 327712 | tf_op jit(solution)/shard_map/ppermute | solution.py:18
  50.6 23.9 %collective-permute-done.1 = bf16[1,80,2048]{2,1,0:T(8,128)(2,1)S(1)} collective-permute-done((bf16[1,80,2048]{2,1,0:T(8,128)(2,1)S(1)}, bf16[1,80,2048]{2,1,0:T(8,128)(2,1)S(1)}, u32[]{:S(2)}, u32[]{:S(2)}) %collective-permute-start.1) | collective-permute-done | bytes 327712 | tf_op jit(solution)/shard_map/ppermute | solution.py:18
  74.7 3.5 %fusion.5 = f32[320,384]{1,0:T(8,128)} fusion(bf16[320,2048]{1,0:T(8,128)(2,1)} %bitcast.3, bf16[1,2048,384]{2,1,0:T(8,128)(2,1)} %all-gather.6.cloned.1.call-done), kind=kOutput, calls=%fused_computation.16 | convolution fusion | flops 503316480 | bytes 3375104 | tf_op jit(solution)/shard_map/dot_general | solution.py:73
  78.2 3.4 %fusion.9 = f32[320,384]{1,0:T(8,128)} fusion(bf16[320,2048]{1,0:T(8,128)(2,1)} %bitcast.3, bf16[1,2048,384]{2,1,0:T(8,128)(2,1)} %all-gather.4.cloned.1.call-done), kind=kOutput, calls=%fused_computation.20 | convolution fusion | flops 503316480 | bytes 3375104 | tf_op jit(solution)/shard_map/dot_general | solution.py:72
  81.6 11.9 %all-gather.8.cloned.1.call-done = bf16[1,384,2048]{2,1,0:T(8,128)(2,1)} async-done(((bf16[1,384,256]{2,1,0:T(8,128)(2,1)}), bf16[1,384,2048]{2,1,0:T(8,128)(2,1)}) %all-gather.8.cloned.1.call-update) | async-done | bytes 1572880 | tf_op jit(solution)/shard_map/all_gather | solution.py:67
  93.4 2.6 %multiply_convert_fusion.2 = (bf16[320,384]{1,0:T(8,128)(2,1)S(1)}, bf16[320,384]{1,0:T(8,128)(2,1)S(1)}, bf16[320,384]{1,0:T(8,128)(2,1)S(1)}) fusion(f32[320,384]{1,0:T(8,128)} %fusion.9, f32[320,384]{1,0:T(8,128)} %fusion.5, bf16[320,2048]{1,0:T(8,128)(2,1)S(1)} %bitcast.74, bf16[1,384,2048]{2,1,0:T(8,128)(2,1)} %all-gather.8.cloned.1.call-done), kind=kOutput, calls=%fused_computation.23 | convolution fusion | flops 505159680 | bytes 4603904 | tf_op jit(solution)/shard_map/dot_general | solution.py:24
  96.1 2.2 convolution_convert_fusion
  98.3 3.6 %convolution_convert_fusion.1 = bf16[2048,384]{1,0:T(8,128)(2,1)} fusion(bf16[320,2048]{1,0:T(8,128)(2,1)} %bitcast.3, bf16[320,384]{1,0:T(8,128)(2,1)S(1)} %get-tuple-element.12), kind=kOutput, calls=%fused_computation.2 | convolution fusion | flops 504102912 | bytes 3129344 | tf_op jit(solution)/shard_map/dot_general | solution.py:30
  104.8 2.1 fusion
  106.8 4.7 %all-to-all-start.2 = ((bf16[4,80,2048]{2,1,0:T(8,128)(2,1)}), bf16[4,80,2048]{2,1,0:T(8,128)(2,1)S(1)}, u32[]{:S(2)}, u32[]{:S(2)}) async-start(bf16[4,80,2048]{2,1,0:T(8,128)(2,1)} %bitcast.12), calls=%async_computation.2 | async-start | bytes 2621440 | tf_op jit(solution)/shard_map/all_to_all | solution.py:112
  111.5 3.3 %convolution_convert_fusion.5 = bf16[320,2048]{1,0:T(8,128)(2,1)} fusion(bf16[320,384]{1,0:T(8,128)(2,1)S(1)} %get-tuple-element.14, bf16[1,384,2048]{2,1,0:T(8,128)(2,1)} %all-gather.8.cloned.1.call-done), kind=kOutput, calls=%fused_computation.7 | convolution fusion | flops 503971840 | bytes 3129344 | tf_op jit(solution)/shard_map/dot_general | solution.py:77
  114.8 28.4 %all-to-all-done.2 = bf16[4,80,2048]{2,1,0:T(8,128)(2,1)S(1)} async-done(((bf16[4,80,2048]{2,1,0:T(8,128)(2,1)}), bf16[4,80,2048]{2,1,0:T(8,128)(2,1)S(1)}, u32[]{:S(2)}, u32[]{:S(2)}) %all-to-all-start.2) | async-done | bytes 1310752 | tf_op jit(solution)/shard_map/all_to_all | solution.py:112
  143.2 4.3 %all-to-all-start.1 = ((bf16[4,80,2048]{2,1,0:T(8,128)(2,1)}), bf16[4,80,2048]{2,1,0:T(8,128)(2,1)}, u32[]{:S(2)}, u32[]{:S(2)}) async-start(bf16[4,80,2048]{2,1,0:T(8,128)(2,1)} %bitcast.7), calls=%async_computation.1 | async-start | bytes 2621440 | tf_op jit(solution)/shard_map/all_to_all | solution.py:78
  147.8 3.7 %convolution_convert_fusion.2 = bf16[2048,384]{1,0:T(8,128)(2,1)} fusion(bf16[320,2048]{1,0:T(8,128)(2,1)} %bitcast.3, bf16[320,384]{1,0:T(8,128)(2,1)S(1)} %get-tuple-element.13), kind=kOutput, calls=%fused_computation.3 | convolution fusion | flops 504102912 | bytes 3129344 | tf_op jit(solution)/shard_map/dot_general | solution.py:30
  154.2 24.3 %all-to-all-done.1 = bf16[4,80,2048]{2,1,0:T(8,128)(2,1)} async-done(((bf16[4,80,2048]{2,1,0:T(8,128)(2,1)}), bf16[4,80,2048]{2,1,0:T(8,128)(2,1)}, u32[]{:S(2)}, u32[]{:S(2)}) %all-to-all-start.1) | async-done | bytes 1310752 | tf_op jit(solution)/shard_map/all_to_all | solution.py:78
  178.5 3.4 %multiply_reduce_fusion = (f32[128,2]{0,1:T(2,128)}, bf16[128,2048]{1,0:T(8,128)(2,1)}) fusion(f32[128,2048]{1,0:T(8,128)} %convert_element_type.67, f32[128,2]{0,1:T(2,128)S(1)} %copy-done.4, bf16[320,2048,1]{1,0,2:T(8,128)(2,1)} %bitcast.9, pred[128,2,320]{2,1,0:T(4,128)(4,1)S(1)} %eq.68), kind=kOutput, calls=%fused_computation.9 | convolution fusion | flops 337379072 | bytes 2967552 | tf_op jit(solution)/shard_map/dot_general | solution.py:30
  181.9 1.7 bitcast_convert_fusion
  183.6 1.7 bitcast_convert_fusion.1
  185.3 34.4 %reduce-scatter.4.cloned.1.call-done = bf16[256,384]{1,0:T(8,128)(2,1)} async-done(((bf16[2048,384]{1,0:T(8,128)(2,1)}), bf16[256,384]{1,0:T(8,128)(2,1)}) %reduce-scatter.4.cloned.1.call-update) | async-done | bytes 196624 | tf_op jit(solution)/shard_map/reduce_scatter | solution.py:99
  (61 shorter events, 16.6 us)
Async XLA Ops:
  7.2 5.9 %copy-start = (bf16[128,2048]{1,0:T(8,128)(2,1)S(1)}, bf16[128,2048]{1,0:T(8,128)(2,1)}, u32[]{:S(2)}) copy-start(bf16[128,2048]{1,0:T(8,128)(2,1)} %param.7) | copy-start | bytes 1572868
  7.2 67.5 %all-gather.6.cloned.1.call-start = ((), (), s32[]{:S(2)}) async-start(), calls=%async_computation.7 | async-start | bytes 1769472 | tf_op jit(solution)/shard_map/all_gather | solution.py:66
  7.9 70.2 %all-gather.4.cloned.1.call-start = ((), (), s32[]{:S(2)}) async-start(), calls=%async_computation.6 | async-start | bytes 1769472 | tf_op jit(solution)/shard_map/all_gather | solution.py:65
  8.7 84.8 %all-gather.8.cloned.1.call-start = ((), (), s32[]{:S(2)}) async-start(), calls=%async_computation.8 | async-start | bytes 1769472 | tf_op jit(solution)/shard_map/all_gather | solution.py:67
  14.7 6.5 %copy-start.1 = (bf16[128,2048]{1,0:T(8,128)(2,1)S(1)}, bf16[128,2048]{1,0:T(8,128)(2,1)}, u32[]{:S(2)}) copy-start(bf16[128,2048]{1,0:T(8,128)(2,1)} %param.10) | copy-start | bytes 1572868
  14.7 60.0 %all-to-all-start = ((bf16[4,80,2048]{2,1,0:T(8,128)(2,1)}), bf16[4,80,2048]{2,1,0:T(8,128)(2,1)}, u32[]{:S(2)}, u32[]{:S(2)}) async-start(bf16[4,80,2048]{2,1,0:T(8,128)(2,1)} %bitcast.2), calls=%async_computation | async-start | bytes 2621440 | tf_op jit(solution)/shard_map/all_to_all | solution.py:62
  21.1 160.8 %reduce-scatter.8.cloned.1.call-start = ((), (), s32[]{:S(2)}) async-start(), calls=%async_computation.11 | async-start | bytes 1769472 | tf_op jit(solution)/shard_map/reduce_scatter | solution.py:105
  22.2 2.5 %copy-start.4 = (f32[128,2]{0,1:T(2,128)S(1)}, f32[128,2]{0,1:T(2,128)}, u32[]{:S(2)}) copy-start(f32[128,2]{0,1:T(2,128)} %param.9) | copy-start | bytes 3076
  27.4 23.1 %collective-permute-start = (bf16[1,80,2048]{2,1,0:T(8,128)(2,1)S(1)}, bf16[1,80,2048]{2,1,0:T(8,128)(2,1)S(1)}, u32[]{:S(2)}, u32[]{:S(2)}) collective-permute-start(bf16[1,80,2048]{2,1,0:T(8,128)(2,1)S(1)} %get-tuple-element.10), channel_id=1, source_target_pairs={{0,1},{1,0},{2,3},{3,2},{4,5},{5,4},{6,7},{7,6},{8,9},{9,8},{10,11... | collective-permute-start | bytes 983048 | tf_op jit(solution)/shard_map/ppermute | solution.py:18
  29.5 45.0 %collective-permute-start.1 = (bf16[1,80,2048]{2,1,0:T(8,128)(2,1)S(1)}, bf16[1,80,2048]{2,1,0:T(8,128)(2,1)S(1)}, u32[]{:S(2)}, u32[]{:S(2)}) collective-permute-start(bf16[1,80,2048]{2,1,0:T(8,128)(2,1)S(1)} %get-tuple-element.9), channel_id=1, source_target_pairs={{0,2},{1,3},{2,0},{3,1},{4,6},{5,7},{6,4},{7,5},{8,10},{9,11},{10,... | collective-permute-start | bytes 983048 | tf_op jit(solution)/shard_map/ppermute | solution.py:18
  31.9 42.7 %collective-permute-start.2 = (bf16[1,80,2048]{2,1,0:T(8,128)(2,1)S(1)}, bf16[1,80,2048]{2,1,0:T(8,128)(2,1)S(1)}, u32[]{:S(2)}, u32[]{:S(2)}) collective-permute-start(bf16[1,80,2048]{2,1,0:T(8,128)(2,1)S(1)} %get-tuple-element.8), channel_id=1, source_target_pairs={{0,3},{1,2},{2,1},{3,0},{4,7},{5,6},{6,5},{7,4},{8,11},{9,10},{10,... | collective-permute-start | bytes 983048 | tf_op jit(solution)/shard_map/ppermute | solution.py:18
  98.2 85.4 %reduce-scatter.6.cloned.1.call-start = ((), (), s32[]{:S(2)}) async-start(), calls=%async_computation.10 | async-start | bytes 1769472 | tf_op jit(solution)/shard_map/reduce_scatter | solution.py:102
  101.9 1.4 copy-start.3
  103.3 1.4 copy-start.2
  106.8 36.4 %all-to-all-start.2 = ((bf16[4,80,2048]{2,1,0:T(8,128)(2,1)}), bf16[4,80,2048]{2,1,0:T(8,128)(2,1)S(1)}, u32[]{:S(2)}, u32[]{:S(2)}) async-start(bf16[4,80,2048]{2,1,0:T(8,128)(2,1)} %bitcast.12), calls=%async_computation.2 | async-start | bytes 2621440 | tf_op jit(solution)/shard_map/all_to_all | solution.py:112
  143.2 35.3 %all-to-all-start.1 = ((bf16[4,80,2048]{2,1,0:T(8,128)(2,1)}), bf16[4,80,2048]{2,1,0:T(8,128)(2,1)}, u32[]{:S(2)}, u32[]{:S(2)}) async-start(bf16[4,80,2048]{2,1,0:T(8,128)(2,1)} %bitcast.7), calls=%async_computation.1 | async-start | bytes 2621440 | tf_op jit(solution)/shard_map/all_to_all | solution.py:78
  147.6 72.2 %reduce-scatter.4.cloned.1.call-start = ((), (), s32[]{:S(2)}) async-start(), calls=%async_computation.9 | async-start | bytes 1769472 | tf_op jit(solution)/shard_map/reduce_scatter | solution.py:99
Sparse Core Ops, SparseCore 0:
  9.9 28.3 all-gather.5
  40.1 25.5 all-gather.3
  67.6 25.7 all-gather.7
  98.4 38.3 reduce-scatter.7
  139.9 38.3 reduce-scatter.5
  181.4 38.3 reduce-scatter.3
